TPU v7x, 32 devices: a whole 2x2x4 slice. The times are simulated.
32 devices in a mesh: lat: 4 (over z), lon: 8 (over y, x, core).
Axes of the slice: x: 2, y: 2, z: 4, core: 2. Of those that a mesh axis runs over, the one named last changes fastest.
Arguments:
- latents: bfloat16 [64, 128, 256], P('lat', 'lon'), may hold values from -6 to 6
- conv_weight: bfloat16 [9, 256, 256], replicated, may hold values from -0.125 to 0.125
- map_weight: bfloat16 [256, 1024], replicated, may hold values from -0.375 to 0.375
- map_bias: float32 [1024], replicated, may hold values from -6 to 6
- input_weight: float32 [3, 512], replicated, may hold values from -3.5 to 3.5
- hidden_weight: bfloat16 [1, 512, 512], replicated, may hold values from -0.25 to 0.25
- output_weight: float32 [512], replicated, may hold values from -0.25 to 0.25
- hit_owner: int32 [768], P(('lat', 'lon')), may hold values from 0 to 31, as said below
- serve_block: int32 [32, 32], P(('lat', 'lon')), may hold values from -1 to 1, as said below
- query_grid: int32 [3, 49152], P(None, ('lat', 'lon')), may hold values from 0 to 127, as said below
- cotangent: float32 [49152], P(('lat', 'lon')), may hold values from -6 to 6
Outputs:
- latent_grad: float32 [64, 128, 256], P('lat', 'lon')
- conv_grad: float32 [9, 256, 256], replicated
- map_grad: float32 [256, 1024], replicated
- map_bias_grad: float32 [1024], replicated
- input_grad: float32 [3, 512], replicated
- hidden_grad: float32 [1, 512, 512], replicated
- output_grad: float32 [512], replicated
Inputs may be any that keep to these rules, and one draw needn't show every extreme that they name: `hit_owner`: each device's 24 entries name distinct devices, numbered lat index times the size of lon plus lon index. `serve_block`: entry [o, r] is a block of device o, 0 to 1, when the list of device r names o, and -1 otherwise. `query_grid`: row 0 is the cell within the block (row-major over 8 rows of 16 cells), row 1 the sub-cell (0 to 35, row-major), row 2 the level (0 to 36).
All inputs are finite; a program needn't handle non-finite values.
Results may differ from a plain program's by a relative error of at most 0.0095.
Values may be sent and summed in bfloat16 or wider, within the bound.
No kernel may reach another device: no remote copies, remote signals or barrier semaphores. Data moves between devices by JAX's collectives and lax.ppermute only.
A program may use at most 128 MiB of HBM per device.

v0:
```python
import jax
import jax.numpy as jnp
from jax import lax
from jax.sharding import PartitionSpec as P

BLOCK = 128
LEVELS = 37
SUB = 6
OMEGA = 30.0


def padded_2(block, sides, width):
    for axis, dim in sides:
        count = lax.axis_size(axis)
        forward = [(i, i + 1) for i in range(count - 1)]
        forward.append((count - 1, 0))
        backward = [(target, source) for source, target in forward]
        low = lax.ppermute(
            lax.slice_in_dim(block, block.shape[dim] - width, None, axis=dim), axis, forward
        )
        high = lax.ppermute(lax.slice_in_dim(block, 0, width, axis=dim), axis, backward)
        block = jnp.concatenate([low, block, high], axis=dim)
    return block


def conv_apply(padded, kernel, row_count, col_count, flipped):
    channels = padded.shape[-1]
    result = jnp.zeros((row_count * col_count, kernel.shape[-1]), jnp.float32)
    for shift_a in (-1, 0, 1):
        for shift_b in (-1, 0, 1):
            tap_index = (shift_a + 1) * 3 + shift_b + 1
            if flipped:
                window = padded[
                    1 - shift_a : 1 - shift_a + row_count, 1 - shift_b : 1 - shift_b + col_count
                ]
                matrix = kernel[tap_index].T
            else:
                window = padded[
                    1 + shift_a : 1 + shift_a + row_count, 1 + shift_b : 1 + shift_b + col_count
                ]
                matrix = kernel[tap_index]
            result = result + jnp.dot(
                window.reshape(row_count * col_count, channels),
                matrix,
                preferred_element_type=jnp.float32,
            )
    return result


def conv_weight_grad(padded, grads, row_count, col_count):
    flat_grads = grads.reshape(row_count * col_count, -1)
    pieces = []
    for shift_a in (-1, 0, 1):
        for shift_b in (-1, 0, 1):
            window = padded[
                1 + shift_a : 1 + shift_a + row_count, 1 + shift_b : 1 + shift_b + col_count
            ]
            window = window.reshape(row_count * col_count, -1)
            pieces.append(jnp.dot(window.T, flat_grads, preferred_element_type=jnp.float32))
    return jnp.stack(pieces)


def close_poles(padded, lat_pos, lat_parts):
    top_rim = jnp.where(lat_pos == 0, jnp.zeros_like(padded[:1]), padded[:1])
    bottom_rim = jnp.where(lat_pos == lat_parts - 1, jnp.zeros_like(padded[-1:]), padded[-1:])
    return jnp.concatenate([top_rim, padded[1:-1], bottom_rim], axis=0)


def split_parts(values):
    upper = values.astype(jnp.bfloat16)
    lower = (values - upper.astype(jnp.float32)).astype(jnp.bfloat16)
    return (upper, lower)


def query_coords(
    cell_index, sub_index, level_index, lat_base, lon_base, lon_tile, lat_cells, lon_cells
):
    row_index = lat_base[:, None] + cell_index // lon_tile
    col_index = lon_base[:, None] + cell_index % lon_tile
    lat_coord = ((row_index * SUB + sub_index // SUB).astype(jnp.float32) + 0.5) / (
        lat_cells * SUB
    ) * 2.0 - 1.0
    lon_coord = ((col_index * SUB + sub_index % SUB).astype(jnp.float32) + 0.5) / (
        lon_cells * SUB
    ) * 2.0 - 1.0
    level_coord = (level_index.astype(jnp.float32) + 0.5) / LEVELS * 2.0 - 1.0
    return jnp.stack([lat_coord.reshape(-1), lon_coord.reshape(-1), level_coord.reshape(-1)])


def sine_grads(
    features, coords, cotan_rows, map_weight, map_bias, input_weight, hidden_weight, output_weight
):
    hidden_size = input_weight.shape[1]
    depth_count = map_weight.shape[1] // hidden_size
    shifts = jnp.dot(features, map_weight, preferred_element_type=jnp.float32) + map_bias
    linear = (
        coords[0][:, None] * input_weight[0]
        + coords[1][:, None] * input_weight[1]
        + coords[2][:, None] * input_weight[2]
    )
    preacts = [OMEGA * linear + shifts[:, :hidden_size]]
    layer_index = 1
    previous = jnp.sin(preacts[-1]).astype(jnp.bfloat16)
    inputs_rounded = [previous]
    preacts.append(
        jnp.dot(previous, hidden_weight[layer_index - 1], preferred_element_type=jnp.float32)
        + shifts[:, layer_index * hidden_size : (layer_index + 1) * hidden_size]
    )
    last_act = jnp.sin(preacts[-1])
    output_grad = jnp.dot(cotan_rows, last_act, precision=lax.Precision.HIGHEST)
    act_grad = cotan_rows[:, None] * output_weight[None, :]
    pre_grads = [None] * depth_count
    rounded_grads = [None] * depth_count
    hidden_grads = [None] * (depth_count - 1)
    for layer_index in range(depth_count - 1, -1, -1):
        pre_grads[layer_index] = act_grad * jnp.cos(preacts[layer_index])
        rounded_grads[layer_index] = pre_grads[layer_index].astype(jnp.bfloat16)
        if layer_index > 0:
            hidden_grads[layer_index - 1] = jnp.dot(
                inputs_rounded[layer_index - 1].T,
                rounded_grads[layer_index],
                preferred_element_type=jnp.float32,
            )
            act_grad = jnp.dot(
                rounded_grads[layer_index],
                hidden_weight[layer_index - 1].T,
                preferred_element_type=jnp.float32,
            )
    input_grad = OMEGA * jnp.dot(coords, pre_grads[0], precision=lax.Precision.HIGHEST)
    mod_grads = jnp.concatenate(rounded_grads, axis=1)
    bias_grad = jnp.sum(jnp.concatenate(pre_grads, axis=1), axis=0)
    map_grad = jnp.dot(features.T, mod_grads, preferred_element_type=jnp.float32)
    feature_grads = jnp.dot(mod_grads, map_weight.T, preferred_element_type=jnp.float32)
    return (feature_grads, (map_grad, bias_grad, input_grad, jnp.stack(hidden_grads), output_grad))


def run_groups(
    blocks,
    cell_index,
    sub_index,
    level_index,
    lat_base,
    lon_base,
    cotan_rows,
    weights,
    lon_tile,
    lat_cells,
    lon_cells,
):
    group_count = blocks.shape[0]
    block_rows = blocks.shape[1]
    channels = blocks.shape[2]
    step_size = 8
    turns = group_count // step_size

    def split_turns(source):
        return source.reshape((turns, step_size) + source.shape[1:])

    inputs = (
        split_turns(blocks),
        split_turns(cell_index),
        split_turns(sub_index),
        split_turns(level_index),
        split_turns(lat_base),
        split_turns(lon_base),
        split_turns(cotan_rows),
    )
    map_weight, map_bias, input_weight, hidden_weight, output_weight = weights
    initial = (
        jnp.zeros(map_weight.shape, jnp.float32),
        jnp.zeros(map_bias.shape, jnp.float32),
        jnp.zeros(input_weight.shape, jnp.float32),
        jnp.zeros(hidden_weight.shape, jnp.float32),
        jnp.zeros(output_weight.shape, jnp.float32),
    )

    def advance(grad_totals, slices):
        block_part, cell_part, sub_part, level_part, latb_part, lonb_part, cotan_part = slices
        onehot = (
            cell_part[:, :, None] == jnp.arange(block_rows, dtype=jnp.int32)[None, None, :]
        ).astype(jnp.bfloat16)
        features_q = jnp.einsum(
            "hgb,hbc->hgc", onehot, block_part, preferred_element_type=jnp.float32
        ).astype(jnp.bfloat16)
        coords = query_coords(
            cell_part, sub_part, level_part, latb_part, lonb_part, lon_tile, lat_cells, lon_cells
        )
        feature_grads, grads = sine_grads(
            features_q.reshape(-1, channels),
            coords,
            cotan_part.reshape(-1),
            map_weight,
            map_bias,
            input_weight,
            hidden_weight,
            output_weight,
        )
        upper, lower = split_parts(
            feature_grads.reshape(onehot.shape[0], onehot.shape[1], channels)
        )
        block_grads = jnp.einsum(
            "hgb,hgc->hbc", onehot, upper, preferred_element_type=jnp.float32
        ) + jnp.einsum("hgb,hgc->hbc", onehot, lower, preferred_element_type=jnp.float32)
        return (jax.tree.map(jnp.add, grad_totals, grads), block_grads)

    grad_totals, block_grads = lax.scan(advance, initial, inputs)
    return (block_grads.reshape(group_count, block_rows, channels), grad_totals)


def on_device(
    latents,
    conv_weight,
    map_weight,
    map_bias,
    input_weight,
    hidden_weight,
    output_weight,
    hit_owner,
    serve_block,
    query_grid,
    cotangent,
):
    lat_tile, lon_tile, channels = latents.shape
    lat_parts = lax.axis_size("lat")
    lon_parts = lax.axis_size("lon")
    dev_count = lat_parts * lon_parts
    lat_cells = lat_tile * lat_parts
    lon_cells = lon_tile * lon_parts
    block_rows = BLOCK
    tile_blocks = lat_tile * lon_tile // block_rows
    rows_per_block = block_rows // lon_tile
    lat_pos = lax.axis_index("lat")
    lon_pos = lax.axis_index("lon")
    padded = close_poles(padded_2(latents, (("lat", 0), ("lon", 1)), 1), lat_pos, lat_parts)
    features = conv_apply(padded, conv_weight, lat_tile, lon_tile, False).astype(jnp.bfloat16)
    own_blocks = features.reshape(tile_blocks, block_rows * channels)
    serve_row = serve_block[0]
    selector = (serve_row[:, None] == jnp.arange(tile_blocks, dtype=jnp.int32)[None, :]).astype(
        jnp.bfloat16
    )
    slot_blocks = jnp.dot(selector, own_blocks, preferred_element_type=jnp.float32).astype(
        jnp.bfloat16
    )
    slot_blocks = slot_blocks.reshape(dev_count, block_rows, channels)
    weights = (map_weight, map_bias, input_weight, hidden_weight, output_weight)
    hit_count = hit_owner.shape[0]
    group_size = cotangent.shape[0] // hit_count
    grid_groups = query_grid.reshape(3, hit_count, group_size).transpose(1, 0, 2)
    grid_slots = jnp.zeros((dev_count, 3, group_size), jnp.int32).at[hit_owner].set(grid_groups)
    cotan_slots = (
        jnp.zeros((dev_count, group_size), jnp.float32)
        .at[hit_owner]
        .set(cotangent.reshape(hit_count, group_size))
    )
    grid_in, cotan_in = (
        lax.all_to_all(grid_slots, ("lat", "lon"), split_axis=0, concat_axis=0, tiled=True),
        lax.all_to_all(cotan_slots, ("lat", "lon"), split_axis=0, concat_axis=0, tiled=True),
    )
    lat_base = lat_pos * lat_tile + serve_row * rows_per_block
    lon_base = jnp.zeros((dev_count,), jnp.int32) + lon_pos * lon_tile
    slot_grads, grad_totals = run_groups(
        slot_blocks,
        grid_in[:, 0],
        grid_in[:, 1],
        grid_in[:, 2],
        lat_base,
        lon_base,
        cotan_in,
        weights,
        lon_tile,
        lat_cells,
        lon_cells,
    )
    slot_upper, slot_lower = split_parts(slot_grads.reshape(dev_count, block_rows * channels))
    tile_grads = jnp.dot(selector.T, slot_upper, preferred_element_type=jnp.float32) + jnp.dot(
        selector.T, slot_lower, preferred_element_type=jnp.float32
    )
    feature_grad = tile_grads.reshape(lat_tile, lon_tile, channels).astype(jnp.bfloat16)
    padded_grad = close_poles(
        padded_2(feature_grad, (("lat", 0), ("lon", 1)), 1), lat_pos, lat_parts
    )
    latent_grad = conv_apply(padded_grad, conv_weight, lat_tile, lon_tile, True).reshape(
        lat_tile, lon_tile, channels
    )
    conv_local = conv_weight_grad(padded, feature_grad, lat_tile, lon_tile)
    totals = lax.psum(
        (
            conv_local,
            grad_totals[0],
            grad_totals[1],
            grad_totals[2],
            grad_totals[3],
            grad_totals[4],
        ),
        ("lat", "lon"),
    )
    grad_scale = float(hit_count * group_size * dev_count) ** (-0.5)
    return (
        latent_grad,
        totals[0] * grad_scale,
        totals[1] * grad_scale,
        totals[2] * grad_scale,
        totals[3] * grad_scale,
        totals[4] * grad_scale,
        totals[5] * grad_scale,
    )


def solution(mesh):
    placed = (
        P("lat", "lon", None),
        P(),
        P(),
        P(),
        P(),
        P(),
        P(),
        P(("lat", "lon")),
        P(("lat", "lon"), None),
        P(None, ("lat", "lon")),
        P(("lat", "lon")),
    )
    return jax.shard_map(
        on_device,
        mesh=mesh,
        in_specs=placed,
        out_specs=(P("lat", "lon", None), P(), P(), P(), P(), P(), P()),
        check_vma=False,
    )
```

profile of v0, /device:TPU:0, one launch (start us, length us, event | category | flops | bytes accessed | tf_op | source)
XLA Modules:
  0.0 379.6 jit_solution(5831723974505579724)
XLA Ops:
  8.0 5.1 %collective-permute-start.1 = (bf16[1,16,256]{2,1,0:T(8,128)(2,1)S(1)}, bf16[1,16,256]{2,1,0:T(8,128)(2,1)S(1)}, u32[]{:S(2)}, u32[]{:S(2)}) collective-permute-start(bf16[1,16,256]{2,1,0:T(8,128)(2,1)S(1)} %get-tuple-element.522), channel_id=1, source_target_pairs={{8,0},{16,8},{24,16},{0,24},{9,1},{17,9},{25,17},{1,25},{10,2},{18... | collective-permute-start | bytes 24584 | tf_op jit(solution)/shard_map/ppermute | solution.py:21
  14.6 1.6 scatter_fusion
  16.9 6.2 %all-to-all-start = ((s32[32,1,192]{2,1,0:T(1,128)}), s32[32,1,192]{2,1,0:T(1,128)}, u32[]{:S(2)}, u32[]{:S(2)}) async-start(s32[32,1,192]{2,1,0:T(1,128)} %reshape.659), calls=%async_computation | async-start | bytes 65536 | tf_op jit(solution)/shard_map/all_to_all | solution.py:256
  23.1 1.2 fusion.80
  25.5 2.5 collective-permute-start.3
  29.5 1.2 scatter_custom_fusion.1
  32.9 2.1 convolution_convert_fusion.1
  34.9 4.9 %all-to-all-start.1 = ((f32[32,1,64]{2,1,0:T(1,128)}), f32[32,1,64]{2,1,0:T(1,128)S(1)}, u32[]{:S(2)}, u32[]{:S(2)}) async-start(f32[32,1,64]{2,1,0:T(1,128)} %bitcast.22), calls=%async_computation.1 | async-start | bytes 32768 | tf_op jit(solution)/shard_map/all_to_all | solution.py:257
  40.4 1.5 reduce.4
  42.0 5.0 %all-to-all-done.1 = f32[32,1,64]{2,1,0:T(1,128)S(1)} async-done(((f32[32,1,64]{2,1,0:T(1,128)}), f32[32,1,64]{2,1,0:T(1,128)S(1)}, u32[]{:S(2)}, u32[]{:S(2)}) %all-to-all-start.1) | async-done | bytes 8224 | tf_op jit(solution)/shard_map/all_to_all | solution.py:257
  47.0 110.0 %while.24 = (s32[]{:T(128)}, f32[256,1024]{1,0:T(8,128)S(1)}, f32[1024]{0:T(1024)S(1)}, f32[3,512]{1,0:T(4,128)}, f32[1,512,512]{2,1,0:T(8,128)}, /*index=5*/f32...) while((s32[]{:T(128)}, f32[256,1024]{1,0:T(8,128)S(1)}, ...), condition=%wide.region_4.5_spmd.clone, body=%wide.region_2.4_spmd.clone.sunk | while | flops 1739577856 | bytes 41995484 | solution.py:206
  49.3 1.1 constant_dynamic-slice_fusion.6
  51.5 7.2 %fusion.204 = (bf16[512,512]{1,0:T(8,128)(2,1)S(1)}, f32[512,512]{1,0:T(8,128)S(1)}, f32[512,512]{1,0:T(8,128)S(1)}) fusion(f32[512]{0:T(512)S(1)} %copy-done.28, f32[512]{0:T(512)S(1)} %mul.582, f32[512,1024]{1,0:T(8,128)S(1)} %convolution_add_fusion.19, bf16[1,512,512]{2,1,0:T(8,128)(2,1)S(1)} %copy-done.27, f32[512]{0:T(512)S(1)} %bitcast.281, ...), kind=kOutput, calls=%fused_computation.233.clone.1 | convolution fusion | flops 271581184 | bytes 5259264 | tf_op jit(solution)/shard_map/while/body/eval_jaxpr/dot_general | solution.py:106
  58.6 4.0 %fusion.208 = f32[1,512]{1,0:T(1,128)S(1)} fusion(f32[512,1]{0,1:T(1,128)S(1)} %reshape.662, f32[512,512]{1,0:T(8,128)S(1)} %get-tuple-element.679), kind=kOutput, calls=%fused_computation.17.clone.1 | convolution fusion | flops 3145728 | bytes 1052672 | tf_op jit(solution)/shard_map/while/body/eval_jaxpr/dot_general | solution.py:110
  62.7 4.1 %fusion.207 = f32[1,512,512]{2,1,0:T(8,128)S(1)} fusion(bf16[512,512]{1,0:T(8,128)(2,1)S(1)} %get-tuple-element.673, f32[1,512,512]{2,1,0:T(8,128)S(1)} %copy-done.4, pred[]{:T(512)S(6)} %compare.35, f32[512,1024]{1,0:T(8,128)S(1)} %convolution_add_fusion.19, f32[512]{0:T(512)S(1)} %bitcast.282, f32[512]{0:T(512)S(1)} %sub.107, ...), kind=kOutput, calls=%fused_computation.11.clone.1 | convolution fusion | flops 271056896 | bytes 3682305 | tf_op jit(solution)/shard_map/while/body/eval_jaxpr/dot_general | solution.py:119
  66.8 3.8 %fusion.205 = (bf16[512,512]{1,0:T(8,128)(2,1)S(1)}, f32[512,512]{1,0:T(8,128)S(1)}) fusion(f32[512,1024]{1,0:T(8,128)S(1)} %convolution_add_fusion.19, f32[512]{0:T(512)S(1)} %bitcast.283, f32[512]{0:T(512)S(1)} %sub.107, f32[512]{0:T(512)S(1)} %bitcast.286, f32[512]{0:T(512)S(1)} %get-tuple-element.670, f32[512]{0:T(512)S(1)} %bitcast.280, ...), kind=kOutput, calls=%fused_computation.235.clone.1 | convolution fusion | flops 270794752 | bytes 3682304 | tf_op jit(solution)/shard_map/while/body/eval_jaxpr/dot_general | solution.py:124
  73.0 1.5 fusion.211
  76.8 1.1 constant_dynamic-slice_fusion.6
  79.0 7.2 %fusion.204 = (bf16[512,512]{1,0:T(8,128)(2,1)S(1)}, f32[512,512]{1,0:T(8,128)S(1)}, f32[512,512]{1,0:T(8,128)S(1)}) fusion(f32[512]{0:T(512)S(1)} %copy-done.28, f32[512]{0:T(512)S(1)} %mul.582, f32[512,1024]{1,0:T(8,128)S(1)} %convolution_add_fusion.19, bf16[1,512,512]{2,1,0:T(8,128)(2,1)S(1)} %copy-done.27, f32[512]{0:T(512)S(1)} %bitcast.281, ...), kind=kOutput, calls=%fused_computation.233.clone.1 | convolution fusion | flops 271581184 | bytes 5259264 | tf_op jit(solution)/shard_map/while/body/eval_jaxpr/dot_general | solution.py:106
  86.2 4.0 %fusion.208 = f32[1,512]{1,0:T(1,128)S(1)} fusion(f32[512,1]{0,1:T(1,128)S(1)} %reshape.662, f32[512,512]{1,0:T(8,128)S(1)} %get-tuple-element.679), kind=kOutput, calls=%fused_computation.17.clone.1 | convolution fusion | flops 3145728 | bytes 1052672 | tf_op jit(solution)/shard_map/while/body/eval_jaxpr/dot_general | solution.py:110
  90.2 4.1 %fusion.207 = f32[1,512,512]{2,1,0:T(8,128)S(1)} fusion(bf16[512,512]{1,0:T(8,128)(2,1)S(1)} %get-tuple-element.673, f32[1,512,512]{2,1,0:T(8,128)S(1)} %copy-done.4, pred[]{:T(512)S(6)} %compare.35, f32[512,1024]{1,0:T(8,128)S(1)} %convolution_add_fusion.19, f32[512]{0:T(512)S(1)} %bitcast.282, f32[512]{0:T(512)S(1)} %sub.107, ...), kind=kOutput, calls=%fused_computation.11.clone.1 | convolution fusion | flops 271056896 | bytes 3682305 | tf_op jit(solution)/shard_map/while/body/eval_jaxpr/dot_general | solution.py:119
  94.3 3.8 %fusion.205 = (bf16[512,512]{1,0:T(8,128)(2,1)S(1)}, f32[512,512]{1,0:T(8,128)S(1)}) fusion(f32[512,1024]{1,0:T(8,128)S(1)} %convolution_add_fusion.19, f32[512]{0:T(512)S(1)} %bitcast.283, f32[512]{0:T(512)S(1)} %sub.107, f32[512]{0:T(512)S(1)} %bitcast.286, f32[512]{0:T(512)S(1)} %get-tuple-element.670, f32[512]{0:T(512)S(1)} %bitcast.280, ...), kind=kOutput, calls=%fused_computation.235.clone.1 | convolution fusion | flops 270794752 | bytes 3682304 | tf_op jit(solution)/shard_map/while/body/eval_jaxpr/dot_general | solution.py:124
  100.5 1.5 fusion.211
  104.3 1.1 constant_dynamic-slice_fusion.6
  106.5 7.2 %fusion.204 = (bf16[512,512]{1,0:T(8,128)(2,1)S(1)}, f32[512,512]{1,0:T(8,128)S(1)}, f32[512,512]{1,0:T(8,128)S(1)}) fusion(f32[512]{0:T(512)S(1)} %copy-done.28, f32[512]{0:T(512)S(1)} %mul.582, f32[512,1024]{1,0:T(8,128)S(1)} %convolution_add_fusion.19, bf16[1,512,512]{2,1,0:T(8,128)(2,1)S(1)} %copy-done.27, f32[512]{0:T(512)S(1)} %bitcast.281, ...), kind=kOutput, calls=%fused_computation.233.clone.1 | convolution fusion | flops 271581184 | bytes 5259264 | tf_op jit(solution)/shard_map/while/body/eval_jaxpr/dot_general | solution.py:106
  113.7 4.0 %fusion.208 = f32[1,512]{1,0:T(1,128)S(1)} fusion(f32[512,1]{0,1:T(1,128)S(1)} %reshape.662, f32[512,512]{1,0:T(8,128)S(1)} %get-tuple-element.679), kind=kOutput, calls=%fused_computation.17.clone.1 | convolution fusion | flops 3145728 | bytes 1052672 | tf_op jit(solution)/shard_map/while/body/eval_jaxpr/dot_general | solution.py:110
  117.7 4.1 %fusion.207 = f32[1,512,512]{2,1,0:T(8,128)S(1)} fusion(bf16[512,512]{1,0:T(8,128)(2,1)S(1)} %get-tuple-element.673, f32[1,512,512]{2,1,0:T(8,128)S(1)} %copy-done.4, pred[]{:T(512)S(6)} %compare.35, f32[512,1024]{1,0:T(8,128)S(1)} %convolution_add_fusion.19, f32[512]{0:T(512)S(1)} %bitcast.282, f32[512]{0:T(512)S(1)} %sub.107, ...), kind=kOutput, calls=%fused_computation.11.clone.1 | convolution fusion | flops 271056896 | bytes 3682305 | tf_op jit(solution)/shard_map/while/body/eval_jaxpr/dot_general | solution.py:119
  121.8 3.8 %fusion.205 = (bf16[512,512]{1,0:T(8,128)(2,1)S(1)}, f32[512,512]{1,0:T(8,128)S(1)}) fusion(f32[512,1024]{1,0:T(8,128)S(1)} %convolution_add_fusion.19, f32[512]{0:T(512)S(1)} %bitcast.283, f32[512]{0:T(512)S(1)} %sub.107, f32[512]{0:T(512)S(1)} %bitcast.286, f32[512]{0:T(512)S(1)} %get-tuple-element.670, f32[512]{0:T(512)S(1)} %bitcast.280, ...), kind=kOutput, calls=%fused_computation.235.clone.1 | convolution fusion | flops 270794752 | bytes 3682304 | tf_op jit(solution)/shard_map/while/body/eval_jaxpr/dot_general | solution.py:124
  128.0 1.5 fusion.211
  131.8 1.1 constant_dynamic-slice_fusion.6
  134.0 7.2 %fusion.204 = (bf16[512,512]{1,0:T(8,128)(2,1)S(1)}, f32[512,512]{1,0:T(8,128)S(1)}, f32[512,512]{1,0:T(8,128)S(1)}) fusion(f32[512]{0:T(512)S(1)} %copy-done.28, f32[512]{0:T(512)S(1)} %mul.582, f32[512,1024]{1,0:T(8,128)S(1)} %convolution_add_fusion.19, bf16[1,512,512]{2,1,0:T(8,128)(2,1)S(1)} %copy-done.27, f32[512]{0:T(512)S(1)} %bitcast.281, ...), kind=kOutput, calls=%fused_computation.233.clone.1 | convolution fusion | flops 271581184 | bytes 5259264 | tf_op jit(solution)/shard_map/while/body/eval_jaxpr/dot_general | solution.py:106
  141.1 4.0 %fusion.208 = f32[1,512]{1,0:T(1,128)S(1)} fusion(f32[512,1]{0,1:T(1,128)S(1)} %reshape.662, f32[512,512]{1,0:T(8,128)S(1)} %get-tuple-element.679), kind=kOutput, calls=%fused_computation.17.clone.1 | convolution fusion | flops 3145728 | bytes 1052672 | tf_op jit(solution)/shard_map/while/body/eval_jaxpr/dot_general | solution.py:110
  145.2 4.1 %fusion.207 = f32[1,512,512]{2,1,0:T(8,128)S(1)} fusion(bf16[512,512]{1,0:T(8,128)(2,1)S(1)} %get-tuple-element.673, f32[1,512,512]{2,1,0:T(8,128)S(1)} %copy-done.4, pred[]{:T(512)S(6)} %compare.35, f32[512,1024]{1,0:T(8,128)S(1)} %convolution_add_fusion.19, f32[512]{0:T(512)S(1)} %bitcast.282, f32[512]{0:T(512)S(1)} %sub.107, ...), kind=kOutput, calls=%fused_computation.11.clone.1 | convolution fusion | flops 271056896 | bytes 3682305 | tf_op jit(solution)/shard_map/while/body/eval_jaxpr/dot_general | solution.py:119
  149.3 3.8 %fusion.205 = (bf16[512,512]{1,0:T(8,128)(2,1)S(1)}, f32[512,512]{1,0:T(8,128)S(1)}) fusion(f32[512,1024]{1,0:T(8,128)S(1)} %convolution_add_fusion.19, f32[512]{0:T(512)S(1)} %bitcast.283, f32[512]{0:T(512)S(1)} %sub.107, f32[512]{0:T(512)S(1)} %bitcast.286, f32[512]{0:T(512)S(1)} %get-tuple-element.670, f32[512]{0:T(512)S(1)} %bitcast.280, ...), kind=kOutput, calls=%fused_computation.235.clone.1 | convolution fusion | flops 270794752 | bytes 3682304 | tf_op jit(solution)/shard_map/while/body/eval_jaxpr/dot_general | solution.py:124
  155.5 1.5 fusion.211
  157.0 5.0 %copy.33 = f32[4,8,128,256]{3,1,2,0:T(8,128)S(1)} copy(f32[4,8,128,256]{3,2,1,0:T(8,128)} %get-tuple-element.323) | data formatting | bytes 8388608
  164.4 38.4 %all-reduce = (f32[1024]{0:T(1024)S(1)}, f32[3,512]{1,0:T(4,128)S(1)}, f32[512]{0:T(512)S(1)}) all-reduce(f32[1024]{0:T(1024)S(1)} %get-tuple-element.325, f32[3,512]{1,0:T(4,128)S(1)} %copy-done.18, f32[512]{0:T(512)S(1)} %copy-done.22), channel_id=1, replica_groups=mesh['lat'=4,'lon'=8] {'lat','lon'}, use_global_device_ids=true, to_apply=%region_7.8 | all-reduce | flops 3072 | bytes 24576 | tf_op jit(solution)/shard_map/psum | solution.py:286
  203.4 1.5 collective-permute-start.4
  205.1 0.9 fusion.54
  206.1 0.9 fusion.53
  209.8 0.9 fusion.49
  213.2 2.3 collective-permute-start.5
  215.5 1.3 collective-permute-done.5
  217.0 2.6 collective-permute-start.7
  224.0 142.8 %all-reduce.4.cloned.1.call-done = (f32[9,256,256]{2,1,0:T(8,128)}, f32[256,1024]{1,0:T(8,128)}, f32[1,512,512]{2,1,0:T(8,128)}) async-done(((f32[9,256,256]{2,1,0:T(8,128)}, f32[256,1024]{1,0:T(8,128)}, f32[1,512,512]{2,1,0:T(8,128)}), (f32[9,256,256]{2,1,0:T(8,128)}, f32[256,1024]{1,0:T(8,128)}, f32[1,512,512]{2,1,0:T(8,128)})) %all-reduce.4.cloned.1.call-update) | async-done | bytes 4456464 | tf_op jit(solution)/shard_map/psum | solution.py:286
  366.8 3.4 broadcast_multiply_fusion
  370.1 1.1 broadcast_multiply_fusion.2
  371.7 1.1 broadcast_multiply_fusion.1
  (342 shorter events, 44.5 us)
Async XLA Ops:
  7.2 23.9 %copy-start.2 = (bf16[9,256,256]{2,1,0:T(8,128)(2,1)S(1)}, bf16[9,256,256]{2,1,0:T(8,128)(2,1)}, u32[]{:S(2)}) copy-start(bf16[9,256,256]{2,1,0:T(8,128)(2,1)} %param.14) | copy-start | bytes 3538948
  8.0 17.2 %collective-permute-start.1 = (bf16[1,16,256]{2,1,0:T(8,128)(2,1)S(1)}, bf16[1,16,256]{2,1,0:T(8,128)(2,1)S(1)}, u32[]{:S(2)}, u32[]{:S(2)}) collective-permute-start(bf16[1,16,256]{2,1,0:T(8,128)(2,1)S(1)} %get-tuple-element.522), channel_id=1, source_target_pairs={{8,0},{16,8},{24,16},{0,24},{9,1},{17,9},{25,17},{1,25},{10,2},{18... | collective-permute-start | bytes 24584 | tf_op jit(solution)/shard_map/ppermute | solution.py:21
  13.1 11.2 %collective-permute-start = (bf16[1,16,256]{2,1,0:T(8,128)(2,1)S(1)}, bf16[1,16,256]{2,1,0:T(8,128)(2,1)S(1)}, u32[]{:S(2)}, u32[]{:S(2)}) collective-permute-start(bf16[1,16,256]{2,1,0:T(8,128)(2,1)S(1)} %get-tuple-element.523), channel_id=1, source_target_pairs={{0,8},{8,16},{16,24},{24,0},{1,9},{9,17},{17,25},{25,1},{2,10},{10... | collective-permute-start | bytes 24584 | tf_op jit(solution)/shard_map/ppermute | solution.py:18
  16.9 18.1 %all-to-all-start = ((s32[32,1,192]{2,1,0:T(1,128)}), s32[32,1,192]{2,1,0:T(1,128)}, u32[]{:S(2)}, u32[]{:S(2)}) async-start(s32[32,1,192]{2,1,0:T(1,128)} %reshape.659), calls=%async_computation | async-start | bytes 65536 | tf_op jit(solution)/shard_map/all_to_all | solution.py:256
  25.2 5.5 %collective-permute-start.2 = (bf16[18,1,256]{2,1,0:T(2,128)(2,1)S(1)}, bf16[18,1,256]{2,1,0:T(2,128)(2,1)S(1)}, u32[]{:S(2)}, u32[]{:S(2)}) collective-permute-start(bf16[18,1,256]{2,1,0:T(2,128)(2,1)S(1)} %get-tuple-element.518), channel_id=1, source_target_pairs={{0,1},{1,2},{2,3},{3,4},{4,5},{5,6},{6,7},{7,0},{8,9},{9,10},{10,1... | collective-permute-start | bytes 27656 | tf_op jit(solution)/shard_map/ppermute | solution.py:18
  25.5 5.3 %collective-permute-start.3 = (bf16[18,1,256]{2,1,0:T(2,128)(2,1)S(1)}, bf16[18,1,256]{2,1,0:T(2,128)(2,1)S(1)}, u32[]{:S(2)}, u32[]{:S(2)}) collective-permute-start(bf16[18,1,256]{2,1,0:T(2,128)(2,1)S(1)} %get-tuple-element.519), channel_id=1, source_target_pairs={{1,0},{2,1},{3,2},{4,3},{5,4},{6,5},{7,6},{0,7},{9,8},{10,9},{11,1... | collective-permute-start | bytes 27656 | tf_op jit(solution)/shard_map/ppermute | solution.py:21
  32.4 14.6 %copy-start.1 = (bf16[256,1024]{1,0:T(8,128)(2,1)S(1)}, bf16[256,1024]{1,0:T(8,128)(2,1)}, u32[]{:S(2)}) copy-start(bf16[256,1024]{1,0:T(8,128)(2,1)} %param.15) | copy-start | bytes 1572868
  34.9 12.0 %all-to-all-start.1 = ((f32[32,1,64]{2,1,0:T(1,128)}), f32[32,1,64]{2,1,0:T(1,128)S(1)}, u32[]{:S(2)}, u32[]{:S(2)}) async-start(f32[32,1,64]{2,1,0:T(1,128)} %bitcast.22), calls=%async_computation.1 | async-start | bytes 32768 | tf_op jit(solution)/shard_map/all_to_all | solution.py:257
  39.8 327.0 %all-reduce.4.cloned.1.call-start = ((), (), s32[]{:S(2)}) async-start(), calls=%async_computation.2 | async-start | bytes 8912896 | tf_op jit(solution)/shard_map/psum | solution.py:286
  47.0 3.7 copy-start.19
  51.4 11.1 %copy-start.20 = (f32[512]{0:T(512)S(1)}, f32[512]{0:T(512)}, u32[]{:S(2)}) copy-start(f32[512]{0:T(512)} %get-tuple-element.706) | copy-start | bytes 6148 | tf_op jit(solution)/shard_map/while
  51.4 11.2 %copy-start.4 = (f32[1,512,512]{2,1,0:T(8,128)S(1)}, f32[1,512,512]{2,1,0:T(8,128)}, u32[]{:S(2)}) copy-start(f32[1,512,512]{2,1,0:T(8,128)} %get-tuple-element.705) | copy-start | bytes 3145732 | tf_op jit(solution)/shard_map/while
  62.7 4.1 %copy-start.21 = (f32[512]{0:T(512)}, f32[512]{0:T(512)S(1)}, u32[]{:S(2)}) copy-start(f32[512]{0:T(512)S(1)} %select_add_fusion.5) | copy-start | bytes 6148 | tf_op jit(solution)/shard_map/while
  66.8 4.0 %copy-start.5 = (f32[1,512,512]{2,1,0:T(8,128)}, f32[1,512,512]{2,1,0:T(8,128)S(1)}, u32[]{:S(2)}) copy-start(f32[1,512,512]{2,1,0:T(8,128)S(1)} %fusion.207) | copy-start | bytes 3145732 | tf_op jit(solution)/shard_map/while
  66.8 4.0 %copy-start.16 = (f32[3,512]{1,0:T(4,128)S(1)}, f32[3,512]{1,0:T(4,128)}, u32[]{:S(2)}) copy-start(f32[3,512]{1,0:T(4,128)} %get-tuple-element.704) | copy-start | bytes 18436 | tf_op jit(solution)/shard_map/while
  72.5 2.1 copy-start.24
  74.5 3.7 copy-start.19
  79.0 11.1 %copy-start.20 = (f32[512]{0:T(512)S(1)}, f32[512]{0:T(512)}, u32[]{:S(2)}) copy-start(f32[512]{0:T(512)} %get-tuple-element.706) | copy-start | bytes 6148 | tf_op jit(solution)/shard_map/while
  79.0 11.2 %copy-start.4 = (f32[1,512,512]{2,1,0:T(8,128)S(1)}, f32[1,512,512]{2,1,0:T(8,128)}, u32[]{:S(2)}) copy-start(f32[1,512,512]{2,1,0:T(8,128)} %get-tuple-element.705) | copy-start | bytes 3145732 | tf_op jit(solution)/shard_map/while
  90.2 4.1 %copy-start.21 = (f32[512]{0:T(512)}, f32[512]{0:T(512)S(1)}, u32[]{:S(2)}) copy-start(f32[512]{0:T(512)S(1)} %select_add_fusion.5) | copy-start | bytes 6148 | tf_op jit(solution)/shard_map/while
  94.3 4.0 %copy-start.5 = (f32[1,512,512]{2,1,0:T(8,128)}, f32[1,512,512]{2,1,0:T(8,128)S(1)}, u32[]{:S(2)}) copy-start(f32[1,512,512]{2,1,0:T(8,128)S(1)} %fusion.207) | copy-start | bytes 3145732 | tf_op jit(solution)/shard_map/while
  94.3 4.0 %copy-start.16 = (f32[3,512]{1,0:T(4,128)S(1)}, f32[3,512]{1,0:T(4,128)}, u32[]{:S(2)}) copy-start(f32[3,512]{1,0:T(4,128)} %get-tuple-element.704) | copy-start | bytes 18436 | tf_op jit(solution)/shard_map/while
  100.0 2.1 copy-start.24
  102.0 3.7 copy-start.19
  106.5 11.1 %copy-start.20 = (f32[512]{0:T(512)S(1)}, f32[512]{0:T(512)}, u32[]{:S(2)}) copy-start(f32[512]{0:T(512)} %get-tuple-element.706) | copy-start | bytes 6148 | tf_op jit(solution)/shard_map/while
  106.5 11.2 %copy-start.4 = (f32[1,512,512]{2,1,0:T(8,128)S(1)}, f32[1,512,512]{2,1,0:T(8,128)}, u32[]{:S(2)}) copy-start(f32[1,512,512]{2,1,0:T(8,128)} %get-tuple-element.705) | copy-start | bytes 3145732 | tf_op jit(solution)/shard_map/while
  117.7 4.1 %copy-start.21 = (f32[512]{0:T(512)}, f32[512]{0:T(512)S(1)}, u32[]{:S(2)}) copy-start(f32[512]{0:T(512)S(1)} %select_add_fusion.5) | copy-start | bytes 6148 | tf_op jit(solution)/shard_map/while
  121.8 4.0 %copy-start.5 = (f32[1,512,512]{2,1,0:T(8,128)}, f32[1,512,512]{2,1,0:T(8,128)S(1)}, u32[]{:S(2)}) copy-start(f32[1,512,512]{2,1,0:T(8,128)S(1)} %fusion.207) | copy-start | bytes 3145732 | tf_op jit(solution)/shard_map/while
  121.8 4.0 %copy-start.16 = (f32[3,512]{1,0:T(4,128)S(1)}, f32[3,512]{1,0:T(4,128)}, u32[]{:S(2)}) copy-start(f32[3,512]{1,0:T(4,128)} %get-tuple-element.704) | copy-start | bytes 18436 | tf_op jit(solution)/shard_map/while
  127.5 2.0 copy-start.24
  129.5 3.7 copy-start.19
  134.0 11.1 %copy-start.20 = (f32[512]{0:T(512)S(1)}, f32[512]{0:T(512)}, u32[]{:S(2)}) copy-start(f32[512]{0:T(512)} %get-tuple-element.706) | copy-start | bytes 6148 | tf_op jit(solution)/shard_map/while
  134.0 11.2 %copy-start.4 = (f32[1,512,512]{2,1,0:T(8,128)S(1)}, f32[1,512,512]{2,1,0:T(8,128)}, u32[]{:S(2)}) copy-start(f32[1,512,512]{2,1,0:T(8,128)} %get-tuple-element.705) | copy-start | bytes 3145732 | tf_op jit(solution)/shard_map/while
  145.2 4.1 %copy-start.21 = (f32[512]{0:T(512)}, f32[512]{0:T(512)S(1)}, u32[]{:S(2)}) copy-start(f32[512]{0:T(512)S(1)} %select_add_fusion.5) | copy-start | bytes 6148 | tf_op jit(solution)/shard_map/while
  149.3 4.0 %copy-start.5 = (f32[1,512,512]{2,1,0:T(8,128)}, f32[1,512,512]{2,1,0:T(8,128)S(1)}, u32[]{:S(2)}) copy-start(f32[1,512,512]{2,1,0:T(8,128)S(1)} %fusion.207) | copy-start | bytes 3145732 | tf_op jit(solution)/shard_map/while
  149.3 4.0 %copy-start.16 = (f32[3,512]{1,0:T(4,128)S(1)}, f32[3,512]{1,0:T(4,128)}, u32[]{:S(2)}) copy-start(f32[3,512]{1,0:T(4,128)} %get-tuple-element.704) | copy-start | bytes 18436 | tf_op jit(solution)/shard_map/while
  155.0 2.0 copy-start.24
  157.0 5.0 %copy-start = (f32[256,1024]{1,0:T(8,128)}, f32[256,1024]{1,0:T(8,128)S(1)}, u32[]{:S(2)}) copy-start(f32[256,1024]{1,0:T(8,128)S(1)} %get-tuple-element.324) | copy-start | bytes 3145732
  157.0 5.0 %copy-start.26 = (s32[1,32]{1,0:T(1,128)S(1)}, s32[1,32]{1,0:T(1,128)}, u32[]{:S(2)}) copy-start(s32[1,32]{1,0:T(1,128)} %param.21) | copy-start | bytes 388
  163.1 42.0 %copy-start.9 = (bf16[16,16,256]{2,1,0:T(8,128)(2,1)S(1)}, bf16[16,16,256]{2,1,0:T(8,128)(2,1)}, u32[]{:S(2)}) copy-start(bf16[16,16,256]{2,1,0:T(8,128)(2,1)} %copy-done.8) | copy-start | bytes 393220
  203.4 3.6 copy-start.15
  203.4 12.1 %collective-permute-start.4 = (bf16[1,16,256]{2,1,0:T(8,128)(2,1)S(1)}, bf16[1,16,256]{2,1,0:T(8,128)(2,1)S(1)}, u32[]{:S(2)}, u32[]{:S(2)}) collective-permute-start(bf16[1,16,256]{2,1,0:T(8,128)(2,1)S(1)} %get-tuple-element.521), channel_id=1, source_target_pairs={{0,8},{8,16},{16,24},{24,0},{1,9},{9,17},{17,25},{25,1},{2,10},{10... | collective-permute-start | bytes 24584 | tf_op jit(solution)/shard_map/ppermute | solution.py:18
  206.1 1.9 copy-start.3
  206.1 2.8 copy-start.13
  213.2 3.7 collective-permute-start.5
  216.9 4.1 %collective-permute-start.6 = (bf16[18,1,256]{2,1,0:T(2,128)(2,1)S(1)}, bf16[18,1,256]{2,1,0:T(2,128)(2,1)S(1)}, u32[]{:S(2)}, u32[]{:S(2)}) collective-permute-start(bf16[18,1,256]{2,1,0:T(2,128)(2,1)S(1)} %get-tuple-element.514), channel_id=1, source_target_pairs={{0,1},{1,2},{2,3},{3,4},{4,5},{5,6},{6,7},{7,0},{8,9},{9,10},{10,1... | collective-permute-start | bytes 27656 | tf_op jit(solution)/shard_map/ppermute | solution.py:18
  217.0 4.1 %collective-permute-start.7 = (bf16[18,1,256]{2,1,0:T(2,128)(2,1)S(1)}, bf16[18,1,256]{2,1,0:T(2,128)(2,1)S(1)}, u32[]{:S(2)}, u32[]{:S(2)}) collective-permute-start(bf16[18,1,256]{2,1,0:T(2,128)(2,1)S(1)} %get-tuple-element.515), channel_id=1, source_target_pairs={{1,0},{2,1},{3,2},{4,3},{5,4},{6,5},{7,6},{0,7},{9,8},{10,9},{11,1... | collective-permute-start | bytes 27656 | tf_op jit(solution)/shard_map/ppermute | solution.py:21
  366.8 3.4 copy-start.7
  (25 other events, 29.4 us)
Sparse Core Ops, SparseCore 0:
  220.4 146.3 all-reduce.3
where the time goes:
time: 381 us; the launch traced here: 380 us
  waiting for transfers between devices  150 us (39%)
  matrix products  110 us (29%)
  blocking collectives  38.4 us (10%)
  local copies, waits for them, and re-layouts  28.1 us (7%)
  starting transfers between devices  25.4 us (7%)
  between operations  14.6 us (4%)
  other arithmetic  12 us (3%)
    psum x1, waiting for transfers between devices, on_device(): lax.psum((conv_local, grad_totals[0], grad_totals[1], grad_totals[2], gra...  143 us
    psum x1, blocking collectives, on_device(): lax.psum((conv_local, grad_totals[0], grad_totals[1], grad_totals[2], gra...  38.4 us
    dot_general x4, matrix products, sine_grads(): jnp.dot(previous, hidden_weight[layer_index - 1], preferred_element_type=...  28.7 us
    dot_general x4, matrix products, sine_grads(): jnp.dot(inputs_rounded[layer_index - 1].T, rounded_grads[layer_index], pr...  16.2 us
    dot_general x4, matrix products, sine_grads(): output_grad = jnp.dot(cotan_rows, last_act, precision=lax.Precision.HIGHEST)  15.8 us
    dot_general x4, matrix products, sine_grads(): jnp.dot(rounded_grads[layer_index], hidden_weight[layer_index - 1].T, pre...  15.3 us
    ppermute x4, starting transfers between devices, padded_2(): lax.ppermute(lax.slice_in_dim(block, 0, width, axis=dim), axis, backward)  12.5 us
    dot_general x9, matrix products, conv_weight_grad(): jnp.dot(window.T, flat_grads, preferred_element_type=jnp.float32)  8.39 us
  transfers between devices with their start and end apart: 11, of which 4 were waited for; matrix products, arithmetic and copies ran while one was open for 7% of the time, Pallas kernels for 0%

commit v1 on v0

--- a/solution.py
+++ b/solution.py
@@ -284,15 +284,18 @@
     )
     conv_local = conv_weight_grad(padded, feature_grad, lat_tile, lon_tile)
     totals = lax.psum(
-        (
-            conv_local,
-            grad_totals[0],
-            grad_totals[1],
-            grad_totals[2],
-            grad_totals[3],
-            grad_totals[4],
+        lax.psum(
+            (
+                conv_local,
+                grad_totals[0],
+                grad_totals[1],
+                grad_totals[2],
+                grad_totals[3],
+                grad_totals[4],
+            ),
+            "lon",
         ),
-        ("lat", "lon"),
+        "lat",
     )
     grad_scale = float(hit_count * group_size * dev_count) ** (-0.5)
     return (

time: 381 us -> 435 us (1.14)
  waiting for transfers between devices: 150 us -> 199 us
  blocking collectives: 38.4 us -> 44.1 us
    psum x0 -> x1, waiting for transfers between devices: none -> 109 us  [on_device(): lax.psum(lax.psum((conv_local, grad_totals[0], grad_totals[1], grad_total...]
    psum x1, waiting for transfers between devices: 143 us -> 80.2 us  [on_device(): lax.psum((conv_local, grad_totals[0], grad_totals[1], grad_totals[2], gra...]
    psum x0 -> x1, blocking collectives: none -> 20.5 us  [on_device(): lax.psum(lax.psum((conv_local, grad_totals[0], grad_totals[1], grad_total...]
    psum x1, blocking collectives: 38.4 us -> 23.7 us  [on_device(): lax.psum((conv_local, grad_totals[0], grad_totals[1], grad_totals[2], gra...]
  transfers between devices with their start and end apart: 11 -> 12, of which waited for: 4 -> 5; matrix products, arithmetic and copies ran while one was open for 7% -> 5% of each run, Pallas kernels for 0% -> 0%
where the time goes in v1:
time: 435 us; the launch traced here: 434 us
  waiting for transfers between devices  199 us (46%)
  matrix products  111 us (26%)
  blocking collectives  44.1 us (10%)
  local copies, waits for them, and re-layouts  28.6 us (7%)
  starting transfers between devices  23.1 us (5%)
  between operations  14.6 us (3%)
  other arithmetic  12.8 us (3%)
    psum x1, waiting for transfers between devices, on_device(): lax.psum(lax.psum((conv_local, grad_totals[0], grad_totals[1], grad_total...  109 us
    psum x1, waiting for transfers between devices, on_device(): lax.psum((conv_local, grad_totals[0], grad_totals[1], grad_totals[2], gra...  80.2 us
    dot_general x4, matrix products, sine_grads(): jnp.dot(previous, hidden_weight[layer_index - 1], preferred_element_type=...  28.7 us
    psum x1, blocking collectives, on_device(): lax.psum((conv_local, grad_totals[0], grad_totals[1], grad_totals[2], gra...  23.7 us
    psum x1, blocking collectives, on_device(): lax.psum(lax.psum((conv_local, grad_totals[0], grad_totals[1], grad_total...  20.5 us
    dot_general x4, matrix products, sine_grads(): jnp.dot(inputs_rounded[layer_index - 1].T, rounded_grads[layer_index], pr...  16.2 us
    dot_general x4, matrix products, sine_grads(): output_grad = jnp.dot(cotan_rows, last_act, precision=lax.Precision.HIGHEST)  15.8 us
    dot_general x4, matrix products, sine_grads(): jnp.dot(rounded_grads[layer_index], hidden_weight[layer_index - 1].T, pre...  15.3 us
  transfers between devices with their start and end apart: 12, of which 5 were waited for; matrix products, arithmetic and copies ran while one was open for 5% of the time, Pallas kernels for 0%

profile of v1, /device:TPU:0, one launch (start us, length us, event | category | flops | bytes accessed | tf_op | source)
XLA Modules:
  0.0 433.7 jit_solution(16693888376495259913)
XLA Ops:
  8.0 5.1 %collective-permute-start.1 = (bf16[1,16,256]{2,1,0:T(8,128)(2,1)S(1)}, bf16[1,16,256]{2,1,0:T(8,128)(2,1)S(1)}, u32[]{:S(2)}, u32[]{:S(2)}) collective-permute-start(bf16[1,16,256]{2,1,0:T(8,128)(2,1)S(1)} %get-tuple-element.528), channel_id=1, source_target_pairs={{8,0},{16,8},{24,16},{0,24},{9,1},{17,9},{25,17},{1,25},{10,2},{18... | collective-permute-start | bytes 24584 | tf_op jit(solution)/shard_map/ppermute | solution.py:21
  14.6 1.6 scatter_fusion
  16.9 6.2 %all-to-all-start = ((s32[32,1,192]{2,1,0:T(1,128)}), s32[32,1,192]{2,1,0:T(1,128)}, u32[]{:S(2)}, u32[]{:S(2)}) async-start(s32[32,1,192]{2,1,0:T(1,128)} %reshape.659), calls=%async_computation | async-start | bytes 65536 | tf_op jit(solution)/shard_map/all_to_all | solution.py:256
  23.1 1.2 fusion.80
  25.5 2.5 collective-permute-start.3
  30.1 1.2 scatter_custom_fusion.1
  34.6 2.7 convolution_convert_fusion.1
  37.4 4.9 %all-to-all-start.1 = ((f32[32,1,64]{2,1,0:T(1,128)}), f32[32,1,64]{2,1,0:T(1,128)S(1)}, u32[]{:S(2)}, u32[]{:S(2)}) async-start(f32[32,1,64]{2,1,0:T(1,128)} %bitcast.22), calls=%async_computation.1 | async-start | bytes 32768 | tf_op jit(solution)/shard_map/all_to_all | solution.py:257
  42.8 1.5 reduce.4
  44.4 5.0 %all-to-all-done.1 = f32[32,1,64]{2,1,0:T(1,128)S(1)} async-done(((f32[32,1,64]{2,1,0:T(1,128)}), f32[32,1,64]{2,1,0:T(1,128)S(1)}, u32[]{:S(2)}, u32[]{:S(2)}) %all-to-all-start.1) | async-done | bytes 8224 | tf_op jit(solution)/shard_map/all_to_all | solution.py:257
  49.4 109.4 %while.24 = (s32[]{:T(128)}, f32[256,1024]{1,0:T(8,128)S(1)}, f32[1024]{0:T(1024)S(1)}, f32[3,512]{1,0:T(4,128)S(1)}, f32[1,512,512]{2,1,0:T(8,128)}, /*index=5*...) while((s32[]{:T(128)}, f32[256,1024]{1,0:T(8,128)S(1)}, ...), condition=%wide.region_4.5_spmd.clone, body=%wide.region_2.4_spmd.clone.sunk | while | flops 1739577856 | bytes 41928784 | solution.py:206
  51.8 1.1 constant_dynamic-slice_fusion.6
  53.9 7.2 %fusion.204 = (bf16[512,512]{1,0:T(8,128)(2,1)S(1)}, f32[512,512]{1,0:T(8,128)S(1)}, f32[512,512]{1,0:T(8,128)S(1)}) fusion(f32[512]{0:T(512)S(1)} %copy-done.25, f32[512]{0:T(512)S(1)} %mul.582, f32[512,1024]{1,0:T(8,128)S(1)} %convolution_add_fusion.19, bf16[1,512,512]{2,1,0:T(8,128)(2,1)S(1)} %copy-done.24, f32[512]{0:T(512)S(1)} %bitcast.281, ...), kind=kOutput, calls=%fused_computation.233.clone.1 | convolution fusion | flops 271581184 | bytes 5259264 | tf_op jit(solution)/shard_map/while/body/eval_jaxpr/dot_general | solution.py:106
  61.1 4.0 fusion.208
  65.2 4.1 fusion.207
  69.3 3.8 fusion.205
  75.4 1.5 fusion.211
  79.1 1.1 constant_dynamic-slice_fusion.6
  81.3 7.2 %fusion.204 = (bf16[512,512]{1,0:T(8,128)(2,1)S(1)}, f32[512,512]{1,0:T(8,128)S(1)}, f32[512,512]{1,0:T(8,128)S(1)}) fusion(f32[512]{0:T(512)S(1)} %copy-done.25, f32[512]{0:T(512)S(1)} %mul.582, f32[512,1024]{1,0:T(8,128)S(1)} %convolution_add_fusion.19, bf16[1,512,512]{2,1,0:T(8,128)(2,1)S(1)} %copy-done.24, f32[512]{0:T(512)S(1)} %bitcast.281, ...), kind=kOutput, calls=%fused_computation.233.clone.1 | convolution fusion | flops 271581184 | bytes 5259264 | tf_op jit(solution)/shard_map/while/body/eval_jaxpr/dot_general | solution.py:106
  88.4 4.0 fusion.208
  92.5 4.1 fusion.207
  96.6 3.8 fusion.205
  102.7 1.5 fusion.211
  106.4 1.1 constant_dynamic-slice_fusion.6
  108.5 7.2 %fusion.204 = (bf16[512,512]{1,0:T(8,128)(2,1)S(1)}, f32[512,512]{1,0:T(8,128)S(1)}, f32[512,512]{1,0:T(8,128)S(1)}) fusion(f32[512]{0:T(512)S(1)} %copy-done.25, f32[512]{0:T(512)S(1)} %mul.582, f32[512,1024]{1,0:T(8,128)S(1)} %convolution_add_fusion.19, bf16[1,512,512]{2,1,0:T(8,128)(2,1)S(1)} %copy-done.24, f32[512]{0:T(512)S(1)} %bitcast.281, ...), kind=kOutput, calls=%fused_computation.233.clone.1 | convolution fusion | flops 271581184 | bytes 5259264 | tf_op jit(solution)/shard_map/while/body/eval_jaxpr/dot_general | solution.py:106
  115.7 4.0 fusion.208
  119.8 4.1 fusion.207
  123.9 3.8 fusion.205
  130.0 1.5 fusion.211
  133.7 1.1 constant_dynamic-slice_fusion.6
  135.9 7.2 %fusion.204 = (bf16[512,512]{1,0:T(8,128)(2,1)S(1)}, f32[512,512]{1,0:T(8,128)S(1)}, f32[512,512]{1,0:T(8,128)S(1)}) fusion(f32[512]{0:T(512)S(1)} %copy-done.25, f32[512]{0:T(512)S(1)} %mul.582, f32[512,1024]{1,0:T(8,128)S(1)} %convolution_add_fusion.19, bf16[1,512,512]{2,1,0:T(8,128)(2,1)S(1)} %copy-done.24, f32[512]{0:T(512)S(1)} %bitcast.281, ...), kind=kOutput, calls=%fused_computation.233.clone.1 | convolution fusion | flops 271581184 | bytes 5259264 | tf_op jit(solution)/shard_map/while/body/eval_jaxpr/dot_general | solution.py:106
  143.0 4.0 fusion.208
  147.1 4.1 fusion.207
  151.2 3.8 fusion.205
  157.3 1.5 fusion.211
  158.8 5.0 %copy.33 = f32[4,8,128,256]{3,1,2,0:T(8,128)S(1)} copy(f32[4,8,128,256]{3,2,1,0:T(8,128)} %get-tuple-element.323) | data formatting | bytes 8388608
  168.1 0.9 fusion.52
  169.0 0.9 fusion.51
  173.8 80.2 %all-reduce.7.cloned.1.call-done = (f32[9,256,256]{2,1,0:T(8,128)}, f32[256,1024]{1,0:T(8,128)}, f32[1,512,512]{2,1,0:T(8,128)}) async-done(((f32[9,256,256]{2,1,0:T(8,128)}, f32[256,1024]{1,0:T(8,128)}, f32[1,512,512]{2,1,0:T(8,128)}), (f32[9,256,256]{2,1,0:T(8,128)}, f32[256,1024]{1,0:T(8,128)}, f32[1,512,512]{2,1,0:T(8,128)})) %all-reduce.7.cloned.1.call-update) | async-done | bytes 4456464 | tf_op jit(solution)/shard_map/psum | solution.py:287
  254.1 1.5 collective-permute-start.4
  255.7 23.7 %all-reduce = (f32[1024]{0:T(1024)S(1)}, f32[3,512]{1,0:T(4,128)S(1)}, f32[512]{0:T(512)S(1)}) all-reduce(f32[1024]{0:T(1024)S(1)} %get-tuple-element.325, f32[3,512]{1,0:T(4,128)S(1)} %get-tuple-element.326, f32[512]{0:T(512)S(1)} %copy-done.22), channel_id=1, replica_groups=mesh['lat'=4,'lon'=8] {'lon'}, use_global_device_ids=true, to_apply=%region_9.10 | all-reduce | flops 3072 | bytes 24576 | tf_op jit(solution)/shard_map/psum | solution.py:287
  279.3 20.5 %all-reduce.2 = (f32[1024]{0:T(1024)S(1)}, f32[3,512]{1,0:T(4,128)S(1)}, f32[512]{0:T(512)S(1)}) all-reduce(f32[1024]{0:T(1024)S(1)} %get-tuple-element.465, f32[3,512]{1,0:T(4,128)S(1)} %get-tuple-element.466, f32[512]{0:T(512)S(1)} %get-tuple-element.467), channel_id=1, replica_groups=mesh['lat'=4,'lon'=8] {'lat'}, use_global_device_ids=true, to_apply=%region_10.11 | all-reduce | flops 3072 | bytes 24576 | tf_op jit(solution)/shard_map/psum | solution.py:286
  301.3 3.9 collective-permute-done.5
  305.3 2.6 collective-permute-start.7
  312.3 108.6 %all-reduce.9.cloned.1.call-done = (f32[9,256,256]{2,1,0:T(8,128)}, f32[256,1024]{1,0:T(8,128)}, f32[1,512,512]{2,1,0:T(8,128)}) async-done(((f32[9,256,256]{2,1,0:T(8,128)}, f32[256,1024]{1,0:T(8,128)}, f32[1,512,512]{2,1,0:T(8,128)}), (f32[9,256,256]{2,1,0:T(8,128)}, f32[256,1024]{1,0:T(8,128)}, f32[1,512,512]{2,1,0:T(8,128)})) %all-reduce.9.cloned.1.call-update) | async-done | bytes 4456464 | tf_op jit(solution)/shard_map/psum | solution.py:286
  420.9 3.4 broadcast_multiply_fusion
  424.2 1.1 broadcast_multiply_fusion.2
  425.8 1.1 broadcast_multiply_fusion.1
  (310 shorter events, 46.8 us)
Async XLA Ops:
  7.2 24.5 %copy-start.2 = (bf16[9,256,256]{2,1,0:T(8,128)(2,1)S(1)}, bf16[9,256,256]{2,1,0:T(8,128)(2,1)}, u32[]{:S(2)}) copy-start(bf16[9,256,256]{2,1,0:T(8,128)(2,1)} %param.14) | copy-start | bytes 3538948
  8.0 17.2 %collective-permute-start.1 = (bf16[1,16,256]{2,1,0:T(8,128)(2,1)S(1)}, bf16[1,16,256]{2,1,0:T(8,128)(2,1)S(1)}, u32[]{:S(2)}, u32[]{:S(2)}) collective-permute-start(bf16[1,16,256]{2,1,0:T(8,128)(2,1)S(1)} %get-tuple-element.528), channel_id=1, source_target_pairs={{8,0},{16,8},{24,16},{0,24},{9,1},{17,9},{25,17},{1,25},{10,2},{18... | collective-permute-start | bytes 24584 | tf_op jit(solution)/shard_map/ppermute | solution.py:21
  13.1 11.2 %collective-permute-start = (bf16[1,16,256]{2,1,0:T(8,128)(2,1)S(1)}, bf16[1,16,256]{2,1,0:T(8,128)(2,1)S(1)}, u32[]{:S(2)}, u32[]{:S(2)}) collective-permute-start(bf16[1,16,256]{2,1,0:T(8,128)(2,1)S(1)} %get-tuple-element.529), channel_id=1, source_target_pairs={{0,8},{8,16},{16,24},{24,0},{1,9},{9,17},{17,25},{25,1},{2,10},{10... | collective-permute-start | bytes 24584 | tf_op jit(solution)/shard_map/ppermute | solution.py:18
  16.9 20.5 %all-to-all-start = ((s32[32,1,192]{2,1,0:T(1,128)}), s32[32,1,192]{2,1,0:T(1,128)}, u32[]{:S(2)}, u32[]{:S(2)}) async-start(s32[32,1,192]{2,1,0:T(1,128)} %reshape.659), calls=%async_computation | async-start | bytes 65536 | tf_op jit(solution)/shard_map/all_to_all | solution.py:256
  25.2 6.1 %collective-permute-start.2 = (bf16[18,1,256]{2,1,0:T(2,128)(2,1)S(1)}, bf16[18,1,256]{2,1,0:T(2,128)(2,1)S(1)}, u32[]{:S(2)}, u32[]{:S(2)}) collective-permute-start(bf16[18,1,256]{2,1,0:T(2,128)(2,1)S(1)} %get-tuple-element.524), channel_id=1, source_target_pairs={{0,1},{1,2},{2,3},{3,4},{4,5},{5,6},{6,7},{7,0},{8,9},{9,10},{10,1... | collective-permute-start | bytes 27656 | tf_op jit(solution)/shard_map/ppermute | solution.py:18
  25.5 5.8 %collective-permute-start.3 = (bf16[18,1,256]{2,1,0:T(2,128)(2,1)S(1)}, bf16[18,1,256]{2,1,0:T(2,128)(2,1)S(1)}, u32[]{:S(2)}, u32[]{:S(2)}) collective-permute-start(bf16[18,1,256]{2,1,0:T(2,128)(2,1)S(1)} %get-tuple-element.525), channel_id=1, source_target_pairs={{1,0},{2,1},{3,2},{4,3},{5,4},{6,5},{7,6},{0,7},{9,8},{10,9},{11,1... | collective-permute-start | bytes 27656 | tf_op jit(solution)/shard_map/ppermute | solution.py:21
  31.6 2.3 copy-start.8
  34.2 15.2 %copy-start.1 = (bf16[256,1024]{1,0:T(8,128)(2,1)S(1)}, bf16[256,1024]{1,0:T(8,128)(2,1)}, u32[]{:S(2)}) copy-start(bf16[256,1024]{1,0:T(8,128)(2,1)} %param.15) | copy-start | bytes 1572868
  34.2 15.2 %copy-start.19 = (f32[1024]{0:T(1024)S(1)}, f32[1024]{0:T(1024)}, u32[]{:S(2)}) copy-start(f32[1024]{0:T(1024)} %param.16) | copy-start | bytes 12292
  34.6 14.8 %copy-start.18 = (f32[3,512]{1,0:T(4,128)S(1)}, f32[3,512]{1,0:T(4,128)}, u32[]{:S(2)}) copy-start(f32[3,512]{1,0:T(4,128)} %param.17) | copy-start | bytes 18436
  37.4 12.1 %all-to-all-start.1 = ((f32[32,1,64]{2,1,0:T(1,128)}), f32[32,1,64]{2,1,0:T(1,128)S(1)}, u32[]{:S(2)}, u32[]{:S(2)}) async-start(f32[32,1,64]{2,1,0:T(1,128)} %bitcast.22), calls=%async_computation.1 | async-start | bytes 32768 | tf_op jit(solution)/shard_map/all_to_all | solution.py:257
  42.2 211.8 %all-reduce.7.cloned.1.call-start = ((), (), s32[]{:S(2)}) async-start(), calls=%async_computation.2 | async-start | bytes 8912896 | tf_op jit(solution)/shard_map/psum | solution.py:287
  52.9 1.0 copy-start.24
  52.9 1.0 copy-start.25
  53.9 11.2 %copy-start.20 = (f32[512]{0:T(512)S(1)}, f32[512]{0:T(512)}, u32[]{:S(2)}) copy-start(f32[512]{0:T(512)} %get-tuple-element.712) | copy-start | bytes 6148 | tf_op jit(solution)/shard_map/while
  53.9 11.2 %copy-start.4 = (f32[1,512,512]{2,1,0:T(8,128)S(1)}, f32[1,512,512]{2,1,0:T(8,128)}, u32[]{:S(2)}) copy-start(f32[1,512,512]{2,1,0:T(8,128)} %get-tuple-element.711) | copy-start | bytes 3145732 | tf_op jit(solution)/shard_map/while
  65.2 4.1 copy-start.21
  69.2 4.0 copy-start.5
  80.2 1.0 copy-start.24
  80.2 1.0 copy-start.25
  81.2 11.2 %copy-start.20 = (f32[512]{0:T(512)S(1)}, f32[512]{0:T(512)}, u32[]{:S(2)}) copy-start(f32[512]{0:T(512)} %get-tuple-element.712) | copy-start | bytes 6148 | tf_op jit(solution)/shard_map/while
  81.2 11.2 %copy-start.4 = (f32[1,512,512]{2,1,0:T(8,128)S(1)}, f32[1,512,512]{2,1,0:T(8,128)}, u32[]{:S(2)}) copy-start(f32[1,512,512]{2,1,0:T(8,128)} %get-tuple-element.711) | copy-start | bytes 3145732 | tf_op jit(solution)/shard_map/while
  92.5 4.1 copy-start.21
  96.6 4.0 copy-start.5
  107.5 1.0 copy-start.24
  108.5 11.2 %copy-start.20 = (f32[512]{0:T(512)S(1)}, f32[512]{0:T(512)}, u32[]{:S(2)}) copy-start(f32[512]{0:T(512)} %get-tuple-element.712) | copy-start | bytes 6148 | tf_op jit(solution)/shard_map/while
  108.5 11.2 %copy-start.4 = (f32[1,512,512]{2,1,0:T(8,128)S(1)}, f32[1,512,512]{2,1,0:T(8,128)}, u32[]{:S(2)}) copy-start(f32[1,512,512]{2,1,0:T(8,128)} %get-tuple-element.711) | copy-start | bytes 3145732 | tf_op jit(solution)/shard_map/while
  119.8 4.1 copy-start.21
  123.9 4.0 copy-start.5
  134.8 1.0 copy-start.24
  135.9 11.2 %copy-start.20 = (f32[512]{0:T(512)S(1)}, f32[512]{0:T(512)}, u32[]{:S(2)}) copy-start(f32[512]{0:T(512)} %get-tuple-element.712) | copy-start | bytes 6148 | tf_op jit(solution)/shard_map/while
  135.9 11.2 %copy-start.4 = (f32[1,512,512]{2,1,0:T(8,128)S(1)}, f32[1,512,512]{2,1,0:T(8,128)}, u32[]{:S(2)}) copy-start(f32[1,512,512]{2,1,0:T(8,128)} %get-tuple-element.711) | copy-start | bytes 3145732 | tf_op jit(solution)/shard_map/while
  147.1 4.1 copy-start.21
  151.2 4.0 copy-start.5
  158.8 5.0 %copy-start = (f32[256,1024]{1,0:T(8,128)}, f32[256,1024]{1,0:T(8,128)S(1)}, u32[]{:S(2)}) copy-start(f32[256,1024]{1,0:T(8,128)S(1)} %get-tuple-element.324) | copy-start | bytes 3145732
  158.8 5.0 %copy-start.23 = (s32[1,32]{1,0:T(1,128)S(1)}, s32[1,32]{1,0:T(1,128)}, u32[]{:S(2)}) copy-start(s32[1,32]{1,0:T(1,128)} %param.21) | copy-start | bytes 388
  164.9 1.3 copy-start.9
  166.2 1.9 copy-start.15
  167.2 1.9 copy-start.3
  167.2 2.8 copy-start.13
  173.7 247.2 %all-reduce.9.cloned.1.call-start = ((), (), s32[]{:S(2)}) async-start(), calls=%async_computation.3 | async-start | bytes 8912896 | tf_op jit(solution)/shard_map/psum | solution.py:286
  254.0 1.7 copy-start.22
  254.1 47.1 %collective-permute-start.4 = (bf16[1,16,256]{2,1,0:T(8,128)(2,1)S(1)}, bf16[1,16,256]{2,1,0:T(8,128)(2,1)S(1)}, u32[]{:S(2)}, u32[]{:S(2)}) collective-permute-start(bf16[1,16,256]{2,1,0:T(8,128)(2,1)S(1)} %get-tuple-element.527), channel_id=1, source_target_pairs={{0,8},{8,16},{16,24},{24,0},{1,9},{9,17},{17,25},{25,1},{2,10},{10... | collective-permute-start | bytes 24584 | tf_op jit(solution)/shard_map/ppermute | solution.py:18
  301.2 3.9 collective-permute-start.5
  305.2 4.1 collective-permute-start.6
  305.3 4.1 collective-permute-start.7
  420.9 3.4 copy-start.7
  424.2 1.6 copy-start.6
  (8 other events, 6.4 us)
Sparse Core Ops, SparseCore 0:
  173.8 80.1 all-reduce.6
  256.5 164.2 all-reduce.8
